TPU v7x, 512 devices: a whole 4x8x8 slice. The times are simulated.
512 devices in a mesh: tm: 64 (over y, x, z_lo), run: 8 (over z_hi, core).
Axes of the slice: x: 4, y: 8, z: 8 (z_hi: 4, z_lo: 2; z = z_hi * 2 + z_lo), core: 2. Of those that a mesh axis runs over, the one named last changes fastest.
Arguments:
- signal: bfloat16 [8, 65536, 256], P('run', 'tm'), may hold values from -6 to 6
- conv_weight: bfloat16 [768, 512], replicated, may hold values from -0.21875 to 0.21875
- conv_bias: float32 [512], replicated, may hold values from -3 to 3
- out_weight: bfloat16 [256, 256], replicated, may hold values from -0.375 to 0.375
- out_bias: float32 [256], replicated, may hold values from -3 to 3
- cotangent: bfloat16 [8, 65536, 256], P('run', 'tm'), may hold values from -8 to 8
Outputs:
- output: bfloat16 [8, 65536, 256], P('run', 'tm')
- grad_signal: bfloat16 [8, 65536, 256], P('run', 'tm')
- grad_conv_weight: float32 [768, 512], replicated
- grad_conv_bias: float32 [512], replicated
- grad_out_weight: float32 [256, 256], replicated
- grad_out_bias: float32 [256], replicated
All inputs are finite; a program needn't handle non-finite values.
Results may differ from a plain program's by a relative error of at most 0.0034.
Values may be sent and summed in bfloat16 or wider, within the bound.
A program may use at most 64 MiB of HBM per device.

v0:
```python
import jax
import jax.numpy as jnp
from jax import lax
from jax.sharding import PartitionSpec as P

DILATION_STEPS = 256
KERNEL_TAPS = 3


def passed_along(array, axis, by):
    size = lax.axis_size(axis)
    pairs = [(i, i + by) for i in range(size) if 0 <= i + by < size]
    return lax.ppermute(array, axis, pairs)


def local(signal, conv_weight, conv_bias, out_weight, out_bias, cotangent):
    device_rows = signal.shape[1]
    channels = signal.shape[2]
    receptive_span = (KERNEL_TAPS - 1) * DILATION_STEPS
    history = passed_along(signal[:, device_rows - receptive_span :, :], "tm", 1)
    padded_input = jnp.concatenate([history, signal], 1)
    tap_stack = jnp.concatenate(
        [
            padded_input[
                :,
                receptive_span
                - kernel_tap_index * DILATION_STEPS : receptive_span
                - kernel_tap_index * DILATION_STEPS
                + device_rows,
            ]
            for kernel_tap_index in range(KERNEL_TAPS)
        ],
        2,
    )
    preact = (
        jnp.einsum("bsk,kn->bsn", tap_stack, conv_weight, preferred_element_type=jnp.float32)
        + conv_bias
    )
    filtered = jnp.tanh(preact[..., :channels])
    gated = jax.nn.sigmoid(preact[..., channels:])
    mixed = (filtered * gated).astype(jnp.bfloat16)
    hidden = (
        jnp.einsum("bsc,cd->bsd", mixed, out_weight, preferred_element_type=jnp.float32) + out_bias
    )
    output = (signal.astype(jnp.float32) + hidden).astype(jnp.bfloat16)
    dmixed = jnp.einsum("bsd,cd->bsc", cotangent, out_weight, preferred_element_type=jnp.float32)
    dpre = jnp.concatenate(
        [dmixed * gated * (1.0 - filtered * filtered), dmixed * filtered * gated * (1.0 - gated)], 2
    ).astype(jnp.bfloat16)
    dstacked = jnp.einsum("bsn,kn->bsk", dpre, conv_weight, preferred_element_type=jnp.float32)
    local_grad = jnp.zeros((signal.shape[0], receptive_span + device_rows, channels), jnp.float32)
    for kernel_tap_index in range(KERNEL_TAPS):
        shifted_slice = dstacked[
            ..., kernel_tap_index * channels : (kernel_tap_index + 1) * channels
        ]
        local_grad = local_grad + jnp.pad(
            shifted_slice,
            (
                (0, 0),
                (
                    receptive_span - kernel_tap_index * DILATION_STEPS,
                    kernel_tap_index * DILATION_STEPS,
                ),
                (0, 0),
            ),
        )
    incoming = passed_along(local_grad[:, :receptive_span].astype(jnp.bfloat16), "tm", -1).astype(
        jnp.float32
    )
    grad_signal = (
        cotangent.astype(jnp.float32)
        + local_grad[:, receptive_span:]
        + jnp.pad(incoming, ((0, 0), (device_rows - receptive_span, 0), (0, 0)))
    )
    grad_signal = grad_signal.astype(jnp.bfloat16)
    grad_conv = jnp.einsum("bsk,bsn->kn", tap_stack, dpre, preferred_element_type=jnp.float32)
    grad_cbias = jnp.sum(dpre.astype(jnp.float32), (0, 1))
    grad_proj = jnp.einsum("bsc,bsd->cd", mixed, cotangent, preferred_element_type=jnp.float32)
    grad_pbias = jnp.sum(cotangent.astype(jnp.float32), (0, 1))
    scale = float(signal.shape[0] * lax.axis_size("run") * device_rows * lax.axis_size("tm")) ** (
        -0.5
    )
    summed = lax.psum((grad_conv, grad_cbias, grad_proj, grad_pbias), ("tm", "run"))
    return (
        output,
        grad_signal,
        summed[0] * scale,
        summed[1] * scale,
        summed[2] * scale,
        summed[3] * scale,
    )


def solution(mesh):
    placed = (P("run", "tm", None), P(), P(), P(), P(), P("run", "tm", None))
    return jax.shard_map(
        local,
        mesh=mesh,
        in_specs=placed,
        out_specs=(P("run", "tm", None), P("run", "tm", None), P(), P(), P(), P()),
        check_vma=False,
    )
```

profile of v0, /device:TPU:1, one launch (start us, length us, event | category | flops | bytes accessed | tf_op | source)
XLA Modules:
  0.0 329.9 jit_solution(11281328637928422365)
XLA Ops:
  7.2 0.0 copy-start
  7.2 0.0 copy-start.2
  7.2 0.0 all-reduce.8.cloned.1.call-start
  7.2 1.1 slice.31
  8.3 4.8 %collective-permute-start = (bf16[1,512,256]{2,1,0:T(8,128)(2,1)S(1)}, bf16[1,512,256]{2,1,0:T(8,128)(2,1)S(1)}, u32[]{:S(2)}, u32[]{:S(2)}) collective-permute-start(bf16[1,512,256]{2,1,0:T(8,128)(2,1)S(1)} %slice.31), channel_id=1, source_target_pairs={{0,8},{8,16},{16,24},{24,32},{32,40},{40,48},{48,56},{56,64},{64,7... | collective-permute-start | bytes 786440 | tf_op jit(solution)/shard_map/ppermute | solution.py:13
  13.2 3.3 collective-permute-done
  16.5 1.1 constant_dynamic-update-slice_fusion
  17.5 0.1 fusion.17
  17.7 0.0 copy-start.1
  17.7 0.0 copy-start.5
  17.7 1.0 add_bitcast_fusion
  18.7 0.8 multiply_convert_fusion.1
  19.5 0.0 copy-start.3
  19.5 0.2 convert_reduce_fusion
  19.8 2.2 fusion.8
  21.9 2.7 convolution_bitcast_fusion
  24.6 1.0 fusion.10
  25.6 2.1 fusion.16
  27.7 0.2 pad_add_fusion
  27.9 0.0 copy-start.7
  27.9 0.7 slice.74
  28.7 1.3 collective-permute-start.1
  30.0 0.0 all-reduce.8.cloned.1.call-update
  30.0 2.2 fusion.2
  32.2 4.4 %collective-permute-done.1 = bf16[1,512,256]{2,1,0:T(8,128)(2,1)} collective-permute-done((bf16[1,512,256]{2,1,0:T(8,128)(2,1)}, bf16[1,512,256]{2,1,0:T(8,128)(2,1)}, u32[]{:S(2)}, u32[]{:S(2)}) %collective-permute-start.1) | collective-permute-done | bytes 262176 | tf_op jit(solution)/shard_map/ppermute | solution.py:13
  36.6 2.0 convert_reduce_fusion.1
  38.6 113.1 %all-reduce.4 = (f32[512]{0:T(512)S(1)}, f32[256]{0:T(256)S(1)}) all-reduce(f32[512]{0:T(512)S(1)} %convert_reduce_fusion, f32[256]{0:T(256)S(1)} %get-tuple-element.18), channel_id=1, replica_groups=mesh['tm'=64,'run'=8] {'tm','run'}, use_global_device_ids=true, to_apply=%region_2.3 | all-reduce | flops 768 | bytes 6144 | tf_op jit(solution)/shard_map/psum | solution.py:83
  151.6 0.6 broadcast_multiply_fusion.3
  152.2 0.6 broadcast_multiply_fusion.2
  152.8 166.8 %all-reduce.8.cloned.1.call-done = (f32[768,512]{1,0:T(8,128)}, f32[256,256]{1,0:T(8,128)}) async-done(((f32[768,512]{1,0:T(8,128)}, f32[256,256]{1,0:T(8,128)}), (f32[768,512]{1,0:T(8,128)}, f32[256,256]{1,0:T(8,128)})) %all-reduce.8.cloned.1.call-update) | async-done | bytes 1835024 | tf_op jit(solution)/shard_map/psum | solution.py:83
  319.5 2.8 broadcast_multiply_fusion
  322.3 0.7 broadcast_multiply_fusion.1
  (11 shorter events, 0.0 us)
Async XLA Ops:
  7.2 10.5 %copy-start = (bf16[768,512]{1,0:T(8,128)(2,1)S(1)}, bf16[768,512]{1,0:T(8,128)(2,1)}, u32[]{:S(2)}) copy-start(bf16[768,512]{1,0:T(8,128)(2,1)} %param.7) | copy-start | bytes 2359300
  7.2 10.5 %copy-start.2 = (bf16[1,1024,256]{2,1,0:T(8,128)(2,1)S(1)}, bf16[1,1024,256]{2,1,0:T(8,128)(2,1)}, u32[]{:S(2)}) copy-start(bf16[1,1024,256]{2,1,0:T(8,128)(2,1)} %param.6) | copy-start | bytes 1572868
  7.2 10.5 %copy-start.6 = (f32[512]{0:T(512)S(1)}, f32[512]{0:T(512)}, u32[]{:S(2)}) copy-start(f32[512]{0:T(512)} %param.8) | copy-start | bytes 6148
  7.2 312.3 %all-reduce.8.cloned.1.call-start = ((), (), s32[]{:S(2)}) async-start(), calls=%async_computation | async-start | bytes 3670016 | tf_op jit(solution)/shard_map/psum | solution.py:83
  8.3 8.1 %collective-permute-start = (bf16[1,512,256]{2,1,0:T(8,128)(2,1)S(1)}, bf16[1,512,256]{2,1,0:T(8,128)(2,1)S(1)}, u32[]{:S(2)}, u32[]{:S(2)}) collective-permute-start(bf16[1,512,256]{2,1,0:T(8,128)(2,1)S(1)} %slice.31), channel_id=1, source_target_pairs={{0,8},{8,16},{16,24},{24,32},{32,40},{40,48},{48,56},{56,64},{64,7... | collective-permute-start | bytes 786440 | tf_op jit(solution)/shard_map/ppermute | solution.py:13
  17.7 1.1 copy-start.1
  17.7 1.1 copy-start.5
  19.5 5.1 %copy-start.3 = (bf16[1024,256]{0,1:T(8,128)(2,1)}, bf16[1024,256]{0,1:T(8,128)(2,1)S(1)}, u32[]{:S(2)}) copy-start(bf16[1024,256]{0,1:T(8,128)(2,1)S(1)} %get-tuple-element.15) | copy-start | bytes 1572868
  27.9 2.1 copy-start.7
  28.7 7.9 %collective-permute-start.1 = (bf16[1,512,256]{2,1,0:T(8,128)(2,1)}, bf16[1,512,256]{2,1,0:T(8,128)(2,1)}, u32[]{:S(2)}, u32[]{:S(2)}) collective-permute-start(bf16[1,512,256]{2,1,0:T(8,128)(2,1)} %slice.74), channel_id=1, source_target_pairs={{8,0},{16,8},{24,16},{32,24},{40,32},{48,40},{56,48},{64,56},{72,6... | collective-permute-start | bytes 786440 | tf_op jit(solution)/shard_map/ppermute | solution.py:13
  319.5 2.8 copy-start.4
Sparse Core Ops, SparseCore 0:
  30.1 289.3 all-reduce.7
where the time goes:
time: 330 us
  waiting for transfers between devices  174 us (53%)
  blocking collectives  113 us (34%)
  between operations  14.2 us (4%)
  matrix products  9.89 us (3%)
  other arithmetic  7.02 us (2%)
  starting transfers between devices  6.16 us (2%)
  local copies, waits for them, and re-layouts  5.08 us (2%)
    psum x1, waiting for transfers between devices, local(): lax.psum((grad_conv, grad_cbias, grad_proj, grad_pbias), ('tm', 'run'))  167 us
    psum x1, blocking collectives, local(): lax.psum((grad_conv, grad_cbias, grad_proj, grad_pbias), ('tm', 'run'))  113 us
    ppermute x2, waiting for transfers between devices, passed_along(): return lax.ppermute(array, axis, pairs)  7.68 us
  transfers between devices with their start and end apart: 3, of which 3 were waited for; matrix products, arithmetic and copies ran while one was open for 2% of the time, Pallas kernels for 0%

commit v1 on v0

--- a/solution.py
+++ b/solution.py
@@ -80,7 +80,8 @@
     scale = float(signal.shape[0] * lax.axis_size("run") * device_rows * lax.axis_size("tm")) ** (
         -0.5
     )
-    summed = lax.psum((grad_conv, grad_cbias, grad_proj, grad_pbias), ("tm", "run"))
+    half = lax.psum((grad_conv, grad_cbias, grad_proj, grad_pbias), "tm")
+    summed = lax.psum(half, "run")
     return (
         output,
         grad_signal,

time: 330 us -> 832 us (2.52)
  waiting for transfers between devices: 174 us -> 580 us
  blocking collectives: 113 us -> 211 us
    psum x1 -> x2, waiting for transfers between devices: 167 us -> 572 us  [the longest x1 572 us: local(): half = lax.psum((grad_conv, grad_cbias, grad_proj, grad_pbias), 'tm')]
    psum x1 -> x2, blocking collectives: 113 us -> 211 us  [the longest x1 126 us: local(): half = lax.psum((grad_conv, grad_cbias, grad_proj, grad_pbias), 'tm')]
  transfers between devices with their start and end apart: 3 -> 4, of which waited for: 3 -> 3; matrix products, arithmetic and copies ran while one was open for 2% -> 1% of each run, Pallas kernels for 0% -> 0%
where the time goes in v1:
time: 832 us; the launch traced here: 828 us
  waiting for transfers between devices  580 us (70%)
  blocking collectives  211 us (25%)
  between operations  14.2 us (2%)
    psum x1, waiting for transfers between devices, local(): half = lax.psum((grad_conv, grad_cbias, grad_proj, grad_pbias), 'tm')  572 us
    psum x1, blocking collectives, local(): half = lax.psum((grad_conv, grad_cbias, grad_proj, grad_pbias), 'tm')  126 us
    psum x1, blocking collectives, local(): summed = lax.psum(half, 'run')  84.9 us
  transfers between devices with their start and end apart: 4, of which 3 were waited for; matrix products, arithmetic and copies ran while one was open for 1% of the time, Pallas kernels for 0%

profile of v1, /device:TPU:1, one launch (start us, length us, event | category | flops | bytes accessed | tf_op | source)
XLA Modules:
  0.0 827.5 jit_solution(1950317493220529019)
XLA Ops:
  7.2 0.0 copy-start
  7.2 0.0 copy-start.2
  7.2 0.0 all-reduce.11.cloned.1.call-start
  7.3 1.1 slice.31
  8.3 4.8 collective-permute-start
  13.2 3.3 collective-permute-done
  16.5 1.1 constant_dynamic-update-slice_fusion
  17.5 0.1 fusion.17
  17.7 0.0 copy-start.1
  17.7 1.0 add_bitcast_fusion
  18.7 0.8 multiply_convert_fusion.1
  19.5 1.0 fusion.10
  20.5 2.2 fusion.8
  22.7 0.0 all-reduce.11.cloned.1.call-update
  22.7 0.0 all-reduce.13.cloned.1.call-start
  22.8 571.7 %all-reduce.11.cloned.1.call-done = (f32[768,512]{1,0:T(8,128)}, f32[256,256]{1,0:T(8,128)}) async-done(((f32[768,512]{1,0:T(8,128)}, f32[256,256]{1,0:T(8,128)}), (f32[768,512]{1,0:T(8,128)}, f32[256,256]{1,0:T(8,128)})) %all-reduce.11.cloned.1.call-update) | async-done | bytes 1835024 | tf_op jit(solution)/shard_map/psum | solution.py:83
  594.5 0.0 all-reduce.13.cloned.1.call-update
  594.5 1.0 convolution_bitcast_fusion
  595.6 0.3 fusion.16
  595.9 0.0 copy-start.6
  595.9 0.2 pad_add_fusion
  596.2 1.3 collective-permute-start.1
  597.5 0.2 convert_reduce_fusion
  597.7 1.2 fusion.2
  598.8 4.8 collective-permute-done.1
  603.7 1.1 convert_reduce_fusion.1
  604.7 126.4 %all-reduce.4 = (f32[512]{0:T(512)S(1)}, f32[256]{0:T(256)S(1)}) all-reduce(f32[512]{0:T(512)S(1)} %convert_reduce_fusion, f32[256]{0:T(256)S(1)} %get-tuple-element.22), channel_id=1, replica_groups=mesh['tm'=64,'run'=8] {'tm'}, use_global_device_ids=true, to_apply=%region_3.4 | all-reduce | flops 768 | bytes 6144 | tf_op jit(solution)/shard_map/psum | solution.py:83
  731.1 84.9 %all-reduce.6 = (f32[512]{0:T(512)S(1)}, f32[256]{0:T(256)S(1)}) all-reduce(f32[512]{0:T(512)S(1)} %get-tuple-element.6, f32[256]{0:T(256)S(1)} %get-tuple-element.7), channel_id=1, replica_groups=mesh['tm'=64,'run'=8] {'run'}, use_global_device_ids=true, to_apply=%region_4.5 | all-reduce | flops 768 | bytes 6144 | tf_op jit(solution)/shard_map/psum | solution.py:84
  816.0 0.6 broadcast_multiply_fusion.3
  816.6 0.6 broadcast_multiply_fusion.2
  817.2 2.8 broadcast_multiply_fusion
  820.0 0.7 broadcast_multiply_fusion.1
  (13 shorter events, 0.1 us)
Async XLA Ops:
  7.2 10.5 %copy-start = (bf16[768,512]{1,0:T(8,128)(2,1)S(1)}, bf16[768,512]{1,0:T(8,128)(2,1)}, u32[]{:S(2)}) copy-start(bf16[768,512]{1,0:T(8,128)(2,1)} %param.7) | copy-start | bytes 2359300
  7.2 10.5 %copy-start.2 = (bf16[1,1024,256]{2,1,0:T(8,128)(2,1)S(1)}, bf16[1,1024,256]{2,1,0:T(8,128)(2,1)}, u32[]{:S(2)}) copy-start(bf16[1,1024,256]{2,1,0:T(8,128)(2,1)} %param.6) | copy-start | bytes 1572868
  7.2 10.5 %copy-start.5 = (f32[512]{0:T(512)S(1)}, f32[512]{0:T(512)}, u32[]{:S(2)}) copy-start(f32[512]{0:T(512)} %param.8) | copy-start | bytes 6148
  7.2 587.3 %all-reduce.11.cloned.1.call-start = ((), (), s32[]{:S(2)}) async-start(), calls=%async_computation | async-start | bytes 3670016 | tf_op jit(solution)/shard_map/psum | solution.py:83
  8.3 8.1 collective-permute-start
  17.7 1.1 copy-start.1
  17.7 1.1 copy-start.4
  22.7 794.4 %all-reduce.13.cloned.1.call-start = ((), (), s32[]{:S(2)}) async-start(), calls=%async_computation.1 | async-start | bytes 3670016 | tf_op jit(solution)/shard_map/psum | solution.py:84
  595.9 1.8 copy-start.6
  596.2 7.5 collective-permute-start.1
  817.2 2.8 copy-start.3
Sparse Core Ops, SparseCore 0:
  22.9 571.6 all-reduce.10
  597.8 128.2 all-reduce.12
